TPU v7x, 512 devices: a whole 4x4x16 slice. The times are simulated.
512 devices in a mesh: grp: 8 (over x, core), own: 64 (over z, y).
Axes of the slice: x: 4, y: 4, z: 16, core: 2. Of those that a mesh axis runs over, the one named last changes fastest.
Arguments:
- features: bfloat16 [131072, 128], P(('grp', 'own')), may hold values from -6 to 6
- scenario_ids: int32 [131072], P(('grp', 'own')), may hold values from 0 to 63, as said below
- labels: int32 [2, 131072], P(None, ('grp', 'own')), may hold values 0 or 1
- counts: int32 [64], replicated, may hold values from 400 to 39999
- scenario_weights: bfloat16 [64, 128, 4096], P('own'), may hold values from -0.5 to 0.5
- shared_weights: bfloat16 [128, 4096], replicated, may hold values from -0.5 to 0.5
- gate_weights: bfloat16 [128, 2], replicated, may hold values from -0.5 to 0.5
- tower_weights: bfloat16 [4096, 256], replicated, may hold values from -0.09375 to 0.09375
- tower_out: bfloat16 [256], replicated, may hold values from -0.5 to 0.5
Outputs:
- logits: float32 [2, 131072], P(None, ('grp', 'own'))
- scenario_grad: float32 [64, 128, 4096], P('own', 'grp')
Inputs may be any that keep to these rules, and one draw needn't show every extreme that they name: `scenario_ids`: among the samples of one device each scenario occurs at most 8 times; in every group of 64 consecutive devices' samples some scenario occurs exactly 8 times on each of the devices.
All inputs are finite; a program needn't handle non-finite values. No bound on the sum of `labels` on one device may be relied on, other than what follows from the above.
Results may differ from a plain program's by a relative error of at most 0.0158.
The roundings to bfloat16 on the way count: a program that leaves them out, or rounds other values in their place, can miss the bound.
Values may be sent and summed in bfloat16 or wider, within the bound.
A program may use at most 64 MiB of HBM per device.

v0:
```python
import jax
import jax.numpy as jnp
from jax import lax
from jax.sharding import PartitionSpec as P


def shards(
    features,
    scenario_ids,
    labels,
    counts,
    scenario_weights,
    shared_weights,
    gate_weights,
    tower_weights,
    tower_out,
):
    tokens = features.shape[0]
    inputs_width = features.shape[1]
    owners = lax.axis_size("own")
    capacity = 2 * tokens // owners
    slots = owners * capacity
    tasks = gate_weights.shape[1]
    tower_width = tower_weights.shape[1] // tasks
    expert_width = tower_weights.shape[0]
    onehot = (scenario_ids[:, None] == jnp.arange(owners, dtype=jnp.int32)[None, :]).astype(
        jnp.int32
    )
    ranks = jnp.sum((jnp.cumsum(onehot, axis=0) - 1) * onehot, axis=1)
    slot_of = scenario_ids * capacity + ranks
    matched = (slot_of[None, :] == jnp.arange(slots, dtype=jnp.int32)[:, None]).astype(jnp.int32)
    token_index = jnp.sum(matched * jnp.arange(tokens, dtype=jnp.int32)[None, :], axis=1)
    source = jnp.where(jnp.sum(matched, axis=1) > 0, token_index, tokens)
    padded_x = jnp.concatenate([features, jnp.zeros((1, inputs_width), jnp.bfloat16)], axis=0)
    outgoing = jnp.take(padded_x, source, axis=0).reshape(owners, capacity, inputs_width)
    expert_w = scenario_weights[0]
    received = lax.all_to_all(outgoing, "own", split_axis=0, concat_axis=0, tiled=True)
    hidden = jnp.maximum(
        jnp.einsum("skd,de->ske", received, expert_w, preferred_element_type=jnp.float32), 0.0
    ).astype(jnp.bfloat16)
    shared_out = jnp.maximum(
        jnp.dot(features, shared_weights, preferred_element_type=jnp.float32), 0.0
    ).astype(jnp.bfloat16)
    shared_proj = jnp.dot(shared_out, tower_weights, preferred_element_type=jnp.float32)
    gate = jax.nn.sigmoid(jnp.dot(features, gate_weights, preferred_element_type=jnp.float32))
    gate_cols = jnp.repeat(gate, tower_width, axis=1)
    arrived = lax.all_to_all(hidden, "own", split_axis=0, concat_axis=0, tiled=True)
    expert_out = jnp.take(arrived.reshape(slots, expert_width), slot_of, axis=0)
    scenario_proj = jnp.dot(expert_out, tower_weights, preferred_element_type=jnp.float32)
    tower_in = gate_cols * scenario_proj + (1.0 - gate_cols) * shared_proj
    tower_act = jnp.maximum(tower_in, 0.0).astype(jnp.bfloat16)
    out_full = tower_out.astype(jnp.float32)
    terms = tower_act.astype(jnp.float32) * out_full[None, :]
    logit_rows = jnp.sum(terms.reshape(tokens, tasks, tower_width), axis=2)
    weight_table = 64.0 / jnp.sqrt(counts.astype(jnp.float32))
    weight = jnp.sum(onehot.astype(jnp.float32) * weight_table[None, :], axis=1)
    dlogit = weight[:, None] * (jax.nn.sigmoid(logit_rows) - labels.T.astype(jnp.float32))
    mixed_grad = jnp.where(
        tower_in > 0.0, gate_cols * jnp.repeat(dlogit, tower_width, axis=1) * out_full[None, :], 0.0
    ).astype(jnp.bfloat16)
    token_grad = lax.dot_general(
        mixed_grad, tower_weights, (((1,), (1,)), ((), ())), preferred_element_type=jnp.float32
    ).astype(jnp.bfloat16)
    padded_token = jnp.concatenate([token_grad, jnp.zeros((1, expert_width), jnp.bfloat16)], axis=0)
    grad_out = jnp.take(padded_token, source, axis=0).reshape(owners, capacity, expert_width)
    expert_grad = lax.all_to_all(grad_out, "own", split_axis=0, concat_axis=0, tiled=True)
    masked = jnp.where(hidden > 0.0, expert_grad, jnp.zeros_like(expert_grad)).reshape(
        slots, expert_width
    )
    inputs_flat = received.reshape(slots, inputs_width)
    shard = lax.psum_scatter(
        lax.dot_general(
            inputs_flat, masked, (((0,), (0,)), ((), ())), preferred_element_type=jnp.float32
        ).astype(jnp.bfloat16),
        "grp",
        scatter_dimension=0,
        tiled=True,
    ).astype(jnp.float32)
    return (logit_rows.T, shard[None])


def solution(mesh):
    return jax.shard_map(
        shards,
        mesh=mesh,
        in_specs=(
            P(("grp", "own"), None),
            P(("grp", "own")),
            P(None, ("grp", "own")),
            P(),
            P("own", None, None),
            P(),
            P(),
            P(),
            P(),
        ),
        out_specs=(P(None, ("grp", "own")), P("own", "grp", None)),
        check_vma=False,
    )
```

profile of v0, /device:TPU:1, one launch (start us, length us, event | category | flops | bytes accessed | tf_op | source)
XLA Modules:
  0.0 512.6 jit_solution(9130660137659916528)
XLA Ops:
  7.2 0.0 copy-start
  7.2 0.8 fusion.22
  8.0 0.6 reduce-window.6
  8.6 0.2 slice_reduce_fusion
  8.9 0.8 fusion.21
  9.7 0.7 compare_and_fusion.1
  10.3 0.2 convert_reduce_fusion
  10.6 0.1 select_n.68
  10.7 0.8 concatenate.6
  11.6 1.3 gather_fusion
  12.9 0.1 bitcast_select_fusion.1
  13.1 34.1 %all_to_all.15 = bf16[64,8,128]{2,1,0:T(8,128)(2,1)S(1)} all-to-all(bf16[64,8,128]{2,1,0:T(8,128)(2,1)S(1)} %bitcast_select_fusion.1), channel_id=1, replica_groups=mesh['grp'=8,'own'=64] {'own'}, dimensions={0} | all-to-all | bytes 262144 | tf_op jit(solution)/shard_map/all_to_all | solution.py:37
  47.2 3.2 maximum_convert_fusion
  50.4 6.7 %all-to-all-start.1 = ((bf16[64,8,4096]{2,1,0:T(8,128)(2,1)}), bf16[64,8,4096]{2,1,0:T(8,128)(2,1)}, u32[]{:S(2)}, u32[]{:S(2)}) async-start(bf16[64,8,4096]{2,1,0:T(8,128)(2,1)} %maximum_convert_fusion), calls=%async_computation.1 | async-start | bytes 8388608 | tf_op jit(solution)/shard_map/all_to_all | solution.py:47
  57.1 0.2 reduce-scatter.2.cloned.1.call-start
  57.3 0.1 fusion.14
  57.5 0.1 bitcast_subtract_fusion
  57.6 0.1 multiply_reduce_fusion
  57.7 181.9 %all-to-all-done.1 = bf16[64,8,4096]{2,1,0:T(8,128)(2,1)} async-done(((bf16[64,8,4096]{2,1,0:T(8,128)(2,1)}), bf16[64,8,4096]{2,1,0:T(8,128)(2,1)}, u32[]{:S(2)}, u32[]{:S(2)}) %all-to-all-start.1) | async-done | bytes 4194336 | tf_op jit(solution)/shard_map/all_to_all | solution.py:47
  239.6 8.0 %gather_fusion.1 = bf16[256,4096]{1,0:T(8,128)(2,1)} fusion(bf16[512,4096]{1,0:T(8,128)(2,1)} %bitcast.8, s32[1024]{0:T(1024)S(1)} %pad_clamp_fusion), kind=kCustom, calls=%fused_computation.1 | custom fusion | bytes 4195328 | tf_op jit(solution)/shard_map/jit(_take)/gather | solution.py:48
  247.6 3.3 fusion.9
  250.9 2.7 bitcast_reduce_fusion
  253.7 0.1 fusion.19
  253.8 0.8 convolution_convert_fusion
  254.6 1.6 concatenate.7
  256.2 10.5 %gather_fusion.2 = bf16[512,4096]{1,0:T(8,128)(2,1)} fusion(bf16[257,4096]{1,0:T(8,128)(2,1)} %concatenate.7, s32[1024]{0:T(1024)S(1)} %pad_clamp_fusion.1), kind=kCustom, calls=%fused_computation.2 | custom fusion | bytes 8390656 | tf_op jit(solution)/shard_map/jit(_take)/gather | solution.py:65
  266.7 2.6 bitcast_select_fusion
  269.3 196.5 %all_to_all.16 = bf16[64,8,4096]{2,1,0:T(8,128)(2,1)S(1)} all-to-all(bf16[64,8,4096]{2,1,0:T(8,128)(2,1)S(1)} %bitcast_select_fusion), channel_id=1, replica_groups=mesh['grp'=8,'own'=64] {'own'}, dimensions={0} | all-to-all | bytes 8388608 | tf_op jit(solution)/shard_map/all_to_all | solution.py:66
  465.8 1.9 fusion.1
  467.7 0.0 reduce-scatter.2.cloned.1.call-update
  467.7 36.4 %reduce-scatter.2.cloned.1.call-done = bf16[16,4096]{1,0:T(8,128)(2,1)} async-done(((bf16[128,4096]{1,0:T(8,128)(2,1)}), bf16[16,4096]{1,0:T(8,128)(2,1)}) %reduce-scatter.2.cloned.1.call-update) | async-done | bytes 131088 | tf_op jit(solution)/shard_map/reduce_scatter | solution.py:71
  504.1 1.6 bitcast_convert_fusion
  (31 shorter events, 0.2 us)
Async XLA Ops:
  7.2 240.5 %copy-start = (bf16[4096,256]{1,0:T(8,128)(2,1)S(1)}, bf16[4096,256]{1,0:T(8,128)(2,1)}, u32[]{:S(2)}) copy-start(bf16[4096,256]{1,0:T(8,128)(2,1)} %param.16) | copy-start | bytes 6291460
  7.2 40.0 %copy-start.2 = (bf16[1,128,4096]{2,1,0:T(8,128)(2,1)S(1)}, bf16[1,128,4096]{2,1,0:T(8,128)(2,1)}, u32[]{:S(2)}) copy-start(bf16[1,128,4096]{2,1,0:T(8,128)(2,1)} %param.13) | copy-start | bytes 3145732
  50.4 6.9 %copy-start.7 = (bf16[256]{0:T(256)(128)(2,1)S(1)}, bf16[256]{0:T(256)(128)(2,1)}, u32[]{:S(2)}) copy-start(bf16[256]{0:T(256)(128)(2,1)} %param.17) | copy-start | bytes 1540
  50.4 6.9 %copy-start.3 = (bf16[256,128]{1,0:T(8,128)(2,1)S(1)}, bf16[256,128]{1,0:T(8,128)(2,1)}, u32[]{:S(2)}) copy-start(bf16[256,128]{1,0:T(8,128)(2,1)} %param.9) | copy-start | bytes 196612
  50.4 7.0 %copy-start.8 = (bf16[128,2]{0,1:T(2,128)(2,1)S(1)}, bf16[128,2]{0,1:T(2,128)(2,1)}, u32[]{:S(2)}) copy-start(bf16[128,2]{0,1:T(2,128)(2,1)} %param.15) | copy-start | bytes 1540
  50.4 7.2 %copy-start.9 = (s32[64]{0:T(128)S(1)}, s32[64]{0:T(128)}, u32[]{:S(2)}) copy-start(s32[64]{0:T(128)} %param.12) | copy-start | bytes 772
  50.4 7.2 %copy-start.4 = (s32[256]{0:T(256)S(1)}, s32[256]{0:T(256)}, u32[]{:S(2)}) copy-start(s32[256]{0:T(256)} %param.10) | copy-start | bytes 3076
  50.4 189.2 %all-to-all-start.1 = ((bf16[64,8,4096]{2,1,0:T(8,128)(2,1)}), bf16[64,8,4096]{2,1,0:T(8,128)(2,1)}, u32[]{:S(2)}, u32[]{:S(2)}) async-start(bf16[64,8,4096]{2,1,0:T(8,128)(2,1)} %maximum_convert_fusion), calls=%async_computation.1 | async-start | bytes 8388608 | tf_op jit(solution)/shard_map/all_to_all | solution.py:47
  57.1 447.1 %reduce-scatter.2.cloned.1.call-start = ((), (), s32[]{:S(2)}) async-start(), calls=%async_computation.4 | async-start | bytes 1179648 | tf_op jit(solution)/shard_map/reduce_scatter | solution.py:71
  250.9 2.7 copy-start.5
  253.6 0.9 copy-start.6
  269.3 196.5 %copy-start.1 = (bf16[64,8,4096]{2,1,0:T(8,128)(2,1)S(1)}, bf16[64,8,4096]{2,1,0:T(8,128)(2,1)}, u32[]{:S(2)}) copy-start(bf16[64,8,4096]{2,1,0:T(8,128)(2,1)} %maximum_convert_fusion) | copy-start | bytes 12582916
Sparse Core Ops, SparseCore 0:
  467.8 36.2 reduce-scatter.1
where the time goes:
time: 514 us; the launch traced here: 513 us
  blocking collectives  231 us (45%)
  waiting for transfers between devices  218 us (42%)
  local copies, waits for them, and re-layouts  22.6 us (4%)
  between operations  14.3 us (3%)
  matrix products  12 us (2%)
  other arithmetic  7.89 us (2%)
  starting transfers between devices  6.88 us (1%)
    all_to_all x1, blocking collectives, shards(): lax.all_to_all(grad_out, 'own', split_axis=0, concat_axis=0, tiled=True)  196 us
    all_to_all x1, waiting for transfers between devices, shards(): lax.all_to_all(hidden, 'own', split_axis=0, concat_axis=0, tiled=True)  182 us
    reduce_scatter x1, waiting for transfers between devices, shards(): lax.psum_scatter(lax.dot_general(inputs_flat, masked, (((0,), (0,)), ((),...  36.4 us
    all_to_all x1, blocking collectives, shards(): lax.all_to_all(outgoing, 'own', split_axis=0, concat_axis=0, tiled=True)  34.1 us
    gather x1, local copies, waits for them, and re-layouts, shards(): jnp.take(padded_token, source, axis=0)  10.5 us
  transfers between devices with their start and end apart: 2, of which 2 were waited for; matrix products, arithmetic and copies ran while one was open for 0% of the time, Pallas kernels for 0%

commit v1 on v0

v1 whole, which is shorter than its diff:
```python
import functools

import jax
import jax.numpy as jnp
from jax import lax
from jax.experimental import pallas as pl
from jax.experimental.pallas import tpu as pltpu
from jax.sharding import PartitionSpec as P

MESH = pl.DeviceIdType.MESH
CAP = 8
LANES = 128
CHUNKS = 4


def dot(a, b, dims=((1,), (0,)), precision=None):
    return lax.dot_general(a, b, (dims, ((), ())), precision=precision, preferred_element_type=jnp.float32)


def iota(shape, dim):
    return lax.broadcasted_iota(jnp.int32, shape, dim)


def step_kernel(
    owners,
    groups,
    ids_ref,
    labels_ref,
    feats_ref,
    counts_ref,
    w_hbm,
    s_hbm,
    gate_ref,
    t_hbm,
    tout_ref,
    logits_ref,
    grad_ref,
    w_ref,
    s_ref,
    t_ref,
    out_x,
    x_ref,
    lab_s,
    lab_r,
    lg_s,
    lg_r,
    hidden,
    proj,
    core_s,
    core_r,
    core_f,
    link_s,
    link_r,
    load_sem,
    x_send,
    x_recv,
    lab_send,
    lab_recv,
    lg_send,
    lg_recv,
    core_send,
    core_recv,
    link_send,
    link_recv,
):
    own = lax.axis_index("own")
    grp = lax.axis_index("grp")
    core = lax.rem(grp, 2)
    chip = lax.div(grp, 2)
    chips = groups // 2
    partner = (grp + 1 - 2 * core, own)
    half = owners // 2
    quarter = owners // 4
    tokens, width = feats_ref.shape
    expert = w_ref.shape[1]
    cols = expert // CHUNKS
    rows = owners * CAP
    part = width // groups

    barrier = pltpu.get_barrier_semaphore()

    def greet(i, carry):
        pl.semaphore_signal(barrier, inc=1, device_id=(grp, lax.rem(own + i, owners)), device_id_type=MESH)
        return carry

    lax.fori_loop(1, owners, greet, 0)
    pl.semaphore_signal(barrier, inc=1, device_id=partner, device_id_type=MESH)
    for d in range(1, chips):
        pl.semaphore_signal(barrier, inc=1, device_id=(lax.rem(grp + 2 * d, groups), own), device_id_type=MESH)

    loads = [
        pltpu.make_async_copy(w_hbm.at[0], w_ref, load_sem.at[0]),
        pltpu.make_async_copy(s_hbm, s_ref, load_sem.at[1]),
        pltpu.make_async_copy(t_hbm, t_ref, load_sem.at[2]),
    ]
    for load in loads:
        load.start()

    ids = ids_ref[...]
    member = iota((owners, tokens), 0) == ids
    member_b = member.astype(jnp.float32).astype(jnp.bfloat16)
    before = (iota((tokens, tokens), 0) < iota((tokens, tokens), 1)).astype(jnp.float32).astype(jnp.bfloat16)
    earlier = dot(member_b, before)
    rank = jnp.sum(jnp.where(member, earlier, 0.0), axis=0, keepdims=True).astype(jnp.int32)
    slot = ids * CAP + rank
    place = (iota((rows, tokens), 0) == slot).astype(jnp.float32).astype(jnp.bfloat16)
    out_x[...] = dot(place, feats_ref[...]).astype(jnp.bfloat16).reshape(owners, CAP, width)
    lane_t = iota((LANES, tokens), 0)
    labels_f = labels_ref[...].astype(jnp.float32)
    label_of = jnp.where(lax.rem(lane_t, 2) == 0, labels_f[0:1], labels_f[1:2])
    label_at = jnp.where(lax.div(lane_t, 2) == rank, label_of, 0.0).astype(jnp.bfloat16)
    lab_s[...] = dot(member_b, label_at, ((1,), (1,))).reshape(owners, 1, LANES)

    pl.semaphore_wait(barrier, owners - 1 + 1 + chips - 1)

    def offset_of(i):
        k = lax.div(i + 1, 2)
        return half - k + 2 * k * lax.rem(i, 2)

    def send_x(group):
        def body(i, carry):
            off = offset_of(i)
            target = lax.rem(own + off, owners)
            spot = lax.rem(owners + quarter - off, owners)
            pltpu.make_async_remote_copy(
                out_x.at[target], x_ref.at[spot], x_send, x_recv.at[group], device_id=(grp, target), device_id_type=MESH
            ).start()
            return carry

        return body

    lax.fori_loop(0, half, send_x(0), 0)
    lax.fori_loop(half, owners - 1, send_x(1), 0)

    def send_label(i, carry):
        off = offset_of(i)
        target = lax.rem(own + off, owners)
        spot = lax.rem(owners + quarter - off, owners)
        pltpu.make_async_remote_copy(
            lab_s.at[target], lab_r.at[spot], lab_send, lab_recv, device_id=(grp, target), device_id_type=MESH
        ).start()
        return carry

    lax.fori_loop(0, owners - 1, send_label, 0)
    x_ref[quarter] = out_x[own]
    lab_r[quarter] = lab_s[own]

    def bulk(src, dst, count, send, recv):
        return pltpu.make_async_remote_copy(
            src.at[pl.ds(0, count)], dst.at[pl.ds(0, count)], send, recv, device_id=partner, device_id_type=MESH
        )

    for load in loads:
        load.wait()

    task_of = lax.div(iota((1, 2 * LANES), 1), LANES)
    gate_b = jnp.where(
        task_of == 0,
        jnp.broadcast_to(gate_ref[:, 0:1].astype(jnp.float32), (width, 2 * LANES)),
        jnp.broadcast_to(gate_ref[:, 1:2].astype(jnp.float32), (width, 2 * LANES)),
    ).astype(jnp.bfloat16)
    tout = tout_ref[...].astype(jnp.float32)
    same_task = lax.div(iota((2 * LANES, 2 * LANES), 0), LANES) == lax.div(iota((2 * LANES, 2 * LANES), 1), LANES)
    tout_b = jnp.where(same_task, tout, 0.0).astype(jnp.bfloat16)

    def forward(group):
        x = x_ref[pl.ds(group * half, half)].reshape(half * CAP, width)
        block = half * CAP
        acc = None
        for c in range(CHUNKS):
            at = pl.ds(c * cols, cols)
            h = jnp.maximum(dot(x, w_ref[:, at]), 0.0).astype(jnp.bfloat16)
            s = jnp.maximum(dot(x, s_ref[:, at]), 0.0).astype(jnp.bfloat16)
            hidden[pl.ds(group * block, block), at] = h
            more = dot(jnp.concatenate([h, s], axis=0), t_ref[at, :])
            acc = more if acc is None else acc + more
        gate = jax.nn.sigmoid(dot(x, gate_b))
        return acc[:block], acc[block:], gate

    bulk(out_x, x_ref, half - 1, x_send, x_recv.at[1]).wait_recv()
    p_near = forward(0)
    bulk(out_x, x_ref, half, x_send, x_recv.at[0]).wait_recv()
    p_far = forward(1)
    scen, shared, gate = (jnp.concatenate([a, b], axis=0) for a, b in zip(p_near, p_far))
    tower_in = gate * scen + (1.0 - gate) * shared
    act = jnp.maximum(tower_in, 0.0).astype(jnp.bfloat16)
    logit = dot(act, tout_b, ((1,), (1,)))

    lane = iota((rows, LANES), 1)
    mine = lax.rem(iota((rows, LANES), 0), CAP) == lax.div(lane, 2)
    pick = jnp.where(lax.rem(lane, 2) == 0, logit[:, :LANES], logit[:, LANES:])
    lg_s[...] = jnp.sum(jnp.where(mine, pick, 0.0).reshape(owners, CAP, LANES), axis=1, keepdims=True)

    def send_logit(i, carry):
        off = offset_of(i)
        target = lax.rem(own + off, owners)
        spot = lax.rem(off + quarter, owners)
        pltpu.make_async_remote_copy(
            lg_s.at[spot], lg_r.at[own], lg_send, lg_recv, device_id=(grp, target), device_id_type=MESH
        ).start()
        return carry

    lax.fori_loop(0, owners - 1, send_logit, 0)
    lg_r[own] = lg_s[quarter]

    bulk(lab_s, lab_r, owners - 1, lab_send, lab_recv).wait_recv()
    spread = (lax.div(iota((rows, owners), 0), CAP) == iota((rows, owners), 1)).astype(jnp.float32).astype(jnp.bfloat16)
    packed = dot(spread, lab_r[...].reshape(owners, LANES).astype(jnp.bfloat16))
    packed = jnp.where(mine, packed, 0.0).astype(jnp.bfloat16)
    fan = (lax.rem(iota((LANES, 2 * LANES), 0), 2) == lax.div(iota((LANES, 2 * LANES), 1), LANES)).astype(jnp.float32).astype(jnp.bfloat16)
    label = dot(packed, fan)
    weight = 64.0 / jnp.sqrt(jnp.full((1, 2 * LANES), counts_ref[own], jnp.int32).astype(jnp.float32))
    dlogit = weight * (jax.nn.sigmoid(logit) - label)
    mixed = jnp.where(tower_in > 0.0, gate * dlogit * tout, 0.0).astype(jnp.bfloat16)

    d_new = iota((width, width), 0)
    d_old = iota((width, width), 1)
    from_row = (2 * lax.rem(lax.div(d_new, part), chips) + lax.div(d_new, part * chips)) * part + lax.rem(d_new, part)
    order = (d_old == from_row).astype(jnp.float32).astype(jnp.bfloat16)
    x_t = dot(order, x_ref[...].reshape(rows, width), ((1,), (1,))).astype(jnp.bfloat16)

    def core_copy(c):
        return pltpu.make_async_remote_copy(
            core_s.at[c, 1 - core], core_r.at[c], core_send.at[c], core_recv.at[c], device_id=partner, device_id_type=MESH
        )

    def link_copy(c, d):
        to = lax.rem(chip + d, chips)
        return pltpu.make_async_remote_copy(
            link_s.at[c, to],
            link_r.at[c, d - 1],
            link_send.at[c, d - 1],
            link_recv.at[c, d - 1],
            device_id=(2 * to + core, own),
            device_id_type=MESH,
        )

    def relay(c):
        core_copy(c).wait_recv()
        total = core_f[c, core] + core_r[c].astype(jnp.float32)
        proj[c] = total.reshape(chips, part, cols)
        link_s[c] = total.astype(jnp.bfloat16).reshape(chips, part, cols)
        for d in (2, 1, 3):
            link_copy(c, d).start()

    for c in range(CHUNKS):
        at = pl.ds(c * cols, cols)
        back = dot(mixed, t_ref[at, :], ((1,), (1,))).astype(jnp.bfloat16)
        masked = jnp.where(hidden[:, at] > 0.0, back, jnp.zeros_like(back))
        share = dot(x_t, masked)
        core_f[c] = share.reshape(2, width // 2, cols)
        core_s[c] = share.astype(jnp.bfloat16).reshape(2, width // 2, cols)
        core_copy(c).start()
        if c > 0:
            relay(c - 1)
    relay(CHUNKS - 1)
    for c in range(CHUNKS):
        total = proj[c, chip]
        for d in range(1, chips):
            link_copy(c, d).wait_recv()
            total = total + link_r[c, d - 1].astype(jnp.float32)
        grad_ref[0, :, pl.ds(c * cols, cols)] = total

    bulk(lg_s, lg_r, owners - 1, lg_send, lg_recv).wait_recv()
    got = lg_r[...].reshape(owners, LANES)
    found = dot(got, member.astype(jnp.float32), ((0,), (0,)), lax.Precision.HIGHEST)
    for task in range(2):
        logits_ref[pl.ds(task, 1), :] = jnp.sum(jnp.where(lane_t == 2 * rank + task, found, 0.0), axis=0, keepdims=True)

    bulk(out_x, x_ref, owners - 1, x_send, x_recv.at[0]).wait_send()
    bulk(lab_s, lab_r, owners - 1, lab_send, lab_recv).wait_send()
    bulk(lg_s, lg_r, owners - 1, lg_send, lg_recv).wait_send()
    for c in range(CHUNKS):
        core_copy(c).wait_send()
        for d in range(1, chips):
            link_copy(c, d).wait_send()


def shards(owners, groups, features, scenario_ids, labels, counts, scenario_weights, shared_weights, gate_weights, tower_weights, tower_out):
    tokens, width = features.shape
    expert, towers = tower_weights.shape
    cols = expert // CHUNKS
    part = width // groups
    chips = groups // 2
    vmem = pl.BlockSpec(memory_space=pltpu.VMEM)
    hbm = pl.BlockSpec(memory_space=pl.ANY)
    dma = pltpu.SemaphoreType.DMA
    bf16, f32 = jnp.bfloat16, jnp.float32
    return pl.pallas_call(
        functools.partial(step_kernel, owners, groups),
        out_shape=(
            jax.ShapeDtypeStruct((2, tokens), f32),
            jax.ShapeDtypeStruct((1, part, expert), f32),
        ),
        in_specs=[vmem, vmem, vmem, pl.BlockSpec(memory_space=pltpu.SMEM), hbm, hbm, vmem, hbm, vmem],
        out_specs=(vmem, vmem),
        scratch_shapes=[
            pltpu.VMEM((width, expert), bf16),
            pltpu.VMEM((width, expert), bf16),
            pltpu.VMEM((expert, towers), bf16),
            pltpu.VMEM((owners, CAP, width), bf16),
            pltpu.VMEM((owners, CAP, width), bf16),
            pltpu.VMEM((owners, 1, LANES), f32),
            pltpu.VMEM((owners, 1, LANES), f32),
            pltpu.VMEM((owners, 1, LANES), f32),
            pltpu.VMEM((owners, 1, LANES), f32),
            pltpu.VMEM((owners * CAP, expert), bf16),
            pltpu.VMEM((CHUNKS, chips, part, cols), f32),
            pltpu.VMEM((CHUNKS, 2, width // 2, cols), bf16),
            pltpu.VMEM((CHUNKS, width // 2, cols), bf16),
            pltpu.VMEM((CHUNKS, 2, width // 2, cols), f32),
            pltpu.VMEM((CHUNKS, chips, part, cols), bf16),
            pltpu.VMEM((CHUNKS, chips - 1, part, cols), bf16),
            dma((3,)),
            dma(()),
            dma((2,)),
            dma(()),
            dma(()),
            dma(()),
            dma(()),
            dma((CHUNKS,)),
            dma((CHUNKS,)),
            dma((CHUNKS, chips - 1)),
            dma((CHUNKS, chips - 1)),
        ],
        compiler_params=pltpu.CompilerParams(collective_id=0, has_side_effects=True, vmem_limit_bytes=56 * 1024 * 1024),
    )(
        scenario_ids.reshape(1, tokens),
        labels,
        features,
        counts,
        scenario_weights,
        shared_weights,
        gate_weights,
        tower_weights,
        tower_out.reshape(1, towers),
    )


def solution(mesh):
    return jax.shard_map(
        functools.partial(shards, mesh.shape["own"], mesh.shape["grp"]),
        mesh=mesh,
        in_specs=(
            P(("grp", "own"), None),
            P(("grp", "own")),
            P(None, ("grp", "own")),
            P(),
            P("own", None, None),
            P(),
            P(),
            P(),
            P(),
        ),
        out_specs=(P(None, ("grp", "own")), P("own", "grp", None)),
        check_vma=False,
    )
```

time: 514 us -> 55.1 us (0.11)
  blocking collectives: 231 us -> 0 us
  waiting for transfers between devices: 218 us -> 0 us
  Pallas kernels: 0 us -> 48.7 us
  local copies, waits for them, and re-layouts: 22.6 us -> 5.52 us
  between operations: 14.3 us -> 0.64 us
  matrix products: 12 us -> 0 us
  other arithmetic: 7.89 us -> 0 us
  starting transfers between devices: 6.88 us -> 0 us
    all_to_all x2 -> x0, blocking collectives: 231 us -> none  [the longest x1 196 us: shards(): lax.all_to_all(grad_out, 'own', split_axis=0, concat_axis=0, tiled=True)]
    all_to_all x1 -> x0, waiting for transfers between devices: 182 us -> none  [shards(): lax.all_to_all(hidden, 'own', split_axis=0, concat_axis=0, tiled=True)]
    pallas_call x0 -> x1, Pallas kernels: none -> 48.7 us  [shards(): pl.pallas_call(functools.partial(step_kernel, owners, groups), out_shape=...]
    reduce_scatter x1 -> x0, waiting for transfers between devices: 36.4 us -> none  [shards(): lax.psum_scatter(lax.dot_general(inputs_flat, masked, (((0,), (0,)), ((),...]
    gather x3 -> x0, local copies, waits for them, and re-layouts: 19.8 us -> none  [the longest x1 10.5 us: shards(): jnp.take(padded_token, source, axis=0)]
    dot_general x6 -> x0, matrix products: 12 us -> none  [the longest x1 3.28 us: shards(): jnp.dot(expert_out, tower_weights, preferred_element_type=jnp.float32)]
    all_to_all x1 -> x0, starting transfers between devices: 6.66 us -> none  [shards(): lax.all_to_all(hidden, 'own', split_axis=0, concat_axis=0, tiled=True)]
  transfers between devices with their start and end apart: 2 -> 0, of which waited for: 2 -> 0; matrix products, arithmetic and copies ran while one was open for 0% -> 0% of each run, Pallas kernels for 0% -> 0%
where the time goes in v1:
time: 55.1 us; the launch traced here: 54.8 us
  Pallas kernels  48.7 us (88%)
  local copies, waits for them, and re-layouts  5.52 us (10%)
  between operations  0.64 us (1%)
    pallas_call x1, Pallas kernels, shards(): pl.pallas_call(functools.partial(step_kernel, owners, groups), out_shape=...  48.7 us
    unnamed x3, local copies, waits for them, and re-layouts  4.3 us
    reshape x1, local copies, waits for them, and re-layouts, shards(): tower_out.reshape(1, towers)  1.22 us

profile of v1, /device:TPU:1, one launch (start us, length us, event | category | flops | bytes accessed | tf_op | source)
XLA Modules:
  0.0 54.8 jit_solution(7829822123359327586)
XLA Ops:
  0.6 1.2 %reshape.11.tout_ref = bf16[1,256]{1,0:T(2,128)(2,1)} reshape(bf16[256]{0:T(256)(128)(2,1)} %param.17) | data formatting | bytes 1024 | tf_op jit(solution)/shard_map/reshape | solution.py:336
  1.8 1.4 %copy.11.gate_ref = bf16[128,2]{1,0:T(8,128)(2,1)} copy(bf16[128,2]{0,1:T(2,128)(2,1)} %param.15) | data formatting | bytes 1024 | tf_op args[6]
  3.2 48.7 %shard_map.104 = (f32[2,256]{1,0:T(2,128)}, f32[1,16,4096]{2,1,0:T(8,128)}) custom-call(s32[1,256]{1,0:T(1,128)} %bitcast.1, s32[2,256]{1,0:T(2,128)} %labels_ref.1, bf16[256,128]{1,0:T(8,128)(2,1)} %feats_ref.1, s32[64]{0:T(128)} %counts_ref.1, bf16[1,128,4096]{2,1,0:T(8,128)(2,1)} %w_hbm.1, bf16[128,4096]{1,0:T(8,128)(2,1)} %s_hbm.1, ...), custom_call_target="tpu_custom_call" | custom-call | tf_op jit(solution)/shard_map/pallas_call | solution.py:289
  51.9 1.2 %copy.14 = f32[2,256]{1,0:T(2,128)} copy(f32[2,256]{1,0:T(2,128)} %get-tuple-element.4) | data formatting | bytes 4096
  53.1 1.7 %copy.15 = f32[1,16,4096]{2,1,0:T(8,128)} copy(f32[1,16,4096]{2,1,0:T(8,128)} %get-tuple-element.5) | data formatting | bytes 524288

commit v2 on v1

--- a/solution.py
+++ b/solution.py
@@ -9,6 +9,8 @@
 
 MESH = pl.DeviceIdType.MESH
 CAP = 8
+YS = 4
+REACH = 4
 LANES = 128
 CHUNKS = 4
 
@@ -58,6 +60,7 @@
     lab_recv,
     lg_send,
     lg_recv,
+    near_sem,
     core_send,
     core_recv,
     link_send,
@@ -69,8 +72,12 @@
     chip = lax.div(grp, 2)
     chips = groups // 2
     partner = (grp + 1 - 2 * core, own)
-    half = owners // 2
-    quarter = owners // 4
+    zs = owners // YS
+    z = lax.div(own, YS)
+    y = lax.rem(own, YS)
+    turn = REACH * YS
+    near = 2 * turn + YS
+    far = owners - near
     tokens, width = feats_ref.shape
     expert = w_ref.shape[1]
     cols = expert // CHUNKS
@@ -79,11 +86,29 @@
 
     barrier = pltpu.get_barrier_semaphore()
 
+    def near_offset(i):
+        k = lax.div(i, 2)
+        off = jnp.where(lax.rem(i, 2) == 0, turn + YS - 1 - k, owners - turn + k)
+        return jnp.where(off == owners, 1, off)
+
+    def far_offset(i):
+        k = lax.div(i, 2)
+        return jnp.where(lax.rem(i, 2) == 0, turn + YS + far // 2 - 1 - k, turn + YS + far // 2 + k)
+
+    def spot_of(off):
+        return lax.rem(off + turn, owners)
+
+    def ahead(off):
+        return lax.rem(z + lax.div(off, YS), zs) * YS + lax.rem(y + lax.rem(off, YS), YS)
+
+    def behind(off):
+        return lax.rem(z + zs - lax.div(off, YS), zs) * YS + lax.rem(y + YS - lax.rem(off, YS), YS)
+
     def greet(i, carry):
-        pl.semaphore_signal(barrier, inc=1, device_id=(grp, lax.rem(own + i, owners)), device_id_type=MESH)
+        pl.semaphore_signal(barrier, inc=1, device_id=(grp, ahead(near_offset(i))), device_id_type=MESH)
         return carry
 
-    lax.fori_loop(1, owners, greet, 0)
+    lax.fori_loop(0, near - 1, greet, 0)
     pl.semaphore_signal(barrier, inc=1, device_id=partner, device_id_type=MESH)
     for d in range(1, chips):
         pl.semaphore_signal(barrier, inc=1, device_id=(lax.rem(grp + 2 * d, groups), own), device_id_type=MESH)
@@ -97,12 +122,15 @@
         load.start()
 
     ids = ids_ref[...]
-    member = iota((owners, tokens), 0) == ids
+    to_z = lax.rem(lax.div(ids, YS) - z + zs, zs)
+    to_y = lax.rem(lax.rem(ids, YS) - y + YS, YS)
+    spots = spot_of(to_z * YS + to_y)
+    member = iota((owners, tokens), 0) == spots
     member_b = member.astype(jnp.float32).astype(jnp.bfloat16)
     before = (iota((tokens, tokens), 0) < iota((tokens, tokens), 1)).astype(jnp.float32).astype(jnp.bfloat16)
     earlier = dot(member_b, before)
     rank = jnp.sum(jnp.where(member, earlier, 0.0), axis=0, keepdims=True).astype(jnp.int32)
-    slot = ids * CAP + rank
+    slot = spots * CAP + rank
     place = (iota((rows, tokens), 0) == slot).astype(jnp.float32).astype(jnp.bfloat16)
     out_x[...] = dot(place, feats_ref[...]).astype(jnp.bfloat16).reshape(owners, CAP, width)
     lane_t = iota((LANES, tokens), 0)
@@ -111,39 +139,38 @@
     label_at = jnp.where(lax.div(lane_t, 2) == rank, label_of, 0.0).astype(jnp.bfloat16)
     lab_s[...] = dot(member_b, label_at, ((1,), (1,))).reshape(owners, 1, LANES)
 
-    pl.semaphore_wait(barrier, owners - 1 + 1 + chips - 1)
-
-    def offset_of(i):
-        k = lax.div(i + 1, 2)
-        return half - k + 2 * k * lax.rem(i, 2)
-
-    def send_x(group):
+    def send_x(offset, group):
         def body(i, carry):
-            off = offset_of(i)
-            target = lax.rem(own + off, owners)
-            spot = lax.rem(owners + quarter - off, owners)
+            off = offset(i)
+            spot = spot_of(off)
             pltpu.make_async_remote_copy(
-                out_x.at[target], x_ref.at[spot], x_send, x_recv.at[group], device_id=(grp, target), device_id_type=MESH
+                out_x.at[spot], x_ref.at[spot], x_send, x_recv.at[group], device_id=(grp, ahead(off)), device_id_type=MESH
             ).start()
             return carry
 
         return body
 
-    lax.fori_loop(0, half, send_x(0), 0)
-    lax.fori_loop(half, owners - 1, send_x(1), 0)
-
-    def send_label(i, carry):
-        off = offset_of(i)
-        target = lax.rem(own + off, owners)
-        spot = lax.rem(owners + quarter - off, owners)
-        pltpu.make_async_remote_copy(
-            lab_s.at[target], lab_r.at[spot], lab_send, lab_recv, device_id=(grp, target), device_id_type=MESH
-        ).start()
-        return carry
-
-    lax.fori_loop(0, owners - 1, send_label, 0)
-    x_ref[quarter] = out_x[own]
-    lab_r[quarter] = lab_s[own]
+    def send_label(offset):
+        def body(i, carry):
+            off = offset(i)
+            spot = spot_of(off)
+            pltpu.make_async_remote_copy(
+                lab_s.at[spot], lab_r.at[spot], lab_send, lab_recv, device_id=(grp, ahead(off)), device_id_type=MESH
+            ).start()
+            return carry
+
+        return body
+
+    pl.semaphore_wait(barrier, near - 1 + 1 + chips - 1)
+    for end in (REACH, zs - REACH):
+        pl.semaphore_signal(near_sem, inc=1, device_id=(grp, lax.rem(z + end, zs) * YS + y), device_id_type=MESH)
+    lax.fori_loop(0, near - 1, send_x(near_offset, 0), 0)
+    pl.semaphore_wait(near_sem, 2)
+    lax.fori_loop(0, far, send_x(far_offset, 1), 0)
+    lax.fori_loop(0, near - 1, send_label(near_offset), 0)
+    lax.fori_loop(0, far, send_label(far_offset), 0)
+    x_ref[turn] = out_x[turn]
+    lab_r[turn] = lab_s[turn]
 
     def bulk(src, dst, count, send, recv):
         return pltpu.make_async_remote_copy(
@@ -153,65 +180,75 @@
     for load in loads:
         load.wait()
 
-    task_of = lax.div(iota((1, 2 * LANES), 1), LANES)
-    gate_b = jnp.where(
-        task_of == 0,
-        jnp.broadcast_to(gate_ref[:, 0:1].astype(jnp.float32), (width, 2 * LANES)),
-        jnp.broadcast_to(gate_ref[:, 1:2].astype(jnp.float32), (width, 2 * LANES)),
-    ).astype(jnp.bfloat16)
-    tout = tout_ref[...].astype(jnp.float32)
+    task_row = lax.div(iota((2 * LANES, 1), 0), LANES)
+    gate_w = gate_ref[...].astype(jnp.float32)
+    gate_b = jnp.where(task_row == 0, gate_w[0:1], gate_w[1:2]).astype(jnp.bfloat16)
+    tout_w = tout_ref[...].astype(jnp.float32)
+    tout = jnp.concatenate([tout_w[0:1], tout_w[1:2]], axis=1)
     same_task = lax.div(iota((2 * LANES, 2 * LANES), 0), LANES) == lax.div(iota((2 * LANES, 2 * LANES), 1), LANES)
     tout_b = jnp.where(same_task, tout, 0.0).astype(jnp.bfloat16)
 
-    def forward(group):
-        x = x_ref[pl.ds(group * half, half)].reshape(half * CAP, width)
-        block = half * CAP
+    def own_lane(blocks):
+        lane = iota((blocks * CAP, LANES), 1)
+        return lane, lax.rem(iota((blocks * CAP, LANES), 0), CAP) == lax.div(lane, 2)
+
+    def forward(first, blocks):
+        x = x_ref[pl.ds(first, blocks)].reshape(blocks * CAP, width)
+        block = blocks * CAP
         acc = None
         for c in range(CHUNKS):
             at = pl.ds(c * cols, cols)
             h = jnp.maximum(dot(x, w_ref[:, at]), 0.0).astype(jnp.bfloat16)
             s = jnp.maximum(dot(x, s_ref[:, at]), 0.0).astype(jnp.bfloat16)
-            hidden[pl.ds(group * block, block), at] = h
+            hidden[pl.ds(first * CAP, block), at] = h
             more = dot(jnp.concatenate([h, s], axis=0), t_ref[at, :])
             acc = more if acc is None else acc + more
-        gate = jax.nn.sigmoid(dot(x, gate_b))
-        return acc[:block], acc[block:], gate
-
-    bulk(out_x, x_ref, half - 1, x_send, x_recv.at[1]).wait_recv()
-    p_near = forward(0)
-    bulk(out_x, x_ref, half, x_send, x_recv.at[0]).wait_recv()
-    p_far = forward(1)
-    scen, shared, gate = (jnp.concatenate([a, b], axis=0) for a, b in zip(p_near, p_far))
-    tower_in = gate * scen + (1.0 - gate) * shared
-    act = jnp.maximum(tower_in, 0.0).astype(jnp.bfloat16)
-    logit = dot(act, tout_b, ((1,), (1,)))
-
-    lane = iota((rows, LANES), 1)
-    mine = lax.rem(iota((rows, LANES), 0), CAP) == lax.div(lane, 2)
-    pick = jnp.where(lax.rem(lane, 2) == 0, logit[:, :LANES], logit[:, LANES:])
-    lg_s[...] = jnp.sum(jnp.where(mine, pick, 0.0).reshape(owners, CAP, LANES), axis=1, keepdims=True)
-
-    def send_logit(i, carry):
-        off = offset_of(i)
-        target = lax.rem(own + off, owners)
-        spot = lax.rem(off + quarter, owners)
-        pltpu.make_async_remote_copy(
-            lg_s.at[spot], lg_r.at[own], lg_send, lg_recv, device_id=(grp, target), device_id_type=MESH
-        ).start()
-        return carry
-
-    lax.fori_loop(0, owners - 1, send_logit, 0)
-    lg_r[own] = lg_s[quarter]
+        gate = jax.nn.sigmoid(dot(x, gate_b, ((1,), (1,))))
+        tower_in = gate * acc[:block] + (1.0 - gate) * acc[block:]
+        act = jnp.maximum(tower_in, 0.0).astype(jnp.bfloat16)
+        logit = dot(act, tout_b, ((1,), (1,)))
+        lane, mine = own_lane(blocks)
+        pick = jnp.where(lax.rem(lane, 2) == 0, logit[:, :LANES], logit[:, LANES:])
+        lg_s[pl.ds(first, blocks)] = jnp.sum(
+            jnp.where(mine, pick, 0.0).reshape(blocks, CAP, LANES), axis=1, keepdims=True
+        )
+        return gate, tower_in, logit
+
+    def send_logit(offset):
+        def body(i, carry):
+            off = offset(i)
+            spot = spot_of(off)
+            pltpu.make_async_remote_copy(
+                lg_s.at[spot], lg_r.at[spot], lg_send, lg_recv, device_id=(grp, behind(off)), device_id_type=MESH
+            ).start()
+            return carry
+
+        return body
+
+    bulk(out_x, x_ref, near - 1, x_send, x_recv.at[0]).wait_recv()
+    near_side = forward(0, near)
+    lax.fori_loop(0, near - 1, send_logit(near_offset), 0)
+    lg_r[turn] = lg_s[turn]
+    bulk(out_x, x_ref, far, x_send, x_recv.at[1]).wait_recv()
+    far_side = forward(near, far)
+    lax.fori_loop(0, far, send_logit(far_offset), 0)
 
     bulk(lab_s, lab_r, owners - 1, lab_send, lab_recv).wait_recv()
     spread = (lax.div(iota((rows, owners), 0), CAP) == iota((rows, owners), 1)).astype(jnp.float32).astype(jnp.bfloat16)
     packed = dot(spread, lab_r[...].reshape(owners, LANES).astype(jnp.bfloat16))
-    packed = jnp.where(mine, packed, 0.0).astype(jnp.bfloat16)
+    packed = jnp.where(own_lane(owners)[1], packed, 0.0).astype(jnp.bfloat16)
     fan = (lax.rem(iota((LANES, 2 * LANES), 0), 2) == lax.div(iota((LANES, 2 * LANES), 1), LANES)).astype(jnp.float32).astype(jnp.bfloat16)
     label = dot(packed, fan)
     weight = 64.0 / jnp.sqrt(jnp.full((1, 2 * LANES), counts_ref[own], jnp.int32).astype(jnp.float32))
-    dlogit = weight * (jax.nn.sigmoid(logit) - label)
-    mixed = jnp.where(tower_in > 0.0, gate * dlogit * tout, 0.0).astype(jnp.bfloat16)
+
+    def gradient(side, label):
+        gate, tower_in, logit = side
+        dlogit = weight * (jax.nn.sigmoid(logit) - label)
+        return jnp.where(tower_in > 0.0, gate * dlogit * tout, 0.0).astype(jnp.bfloat16)
+
+    mixed = jnp.concatenate(
+        [gradient(near_side, label[: near * CAP]), gradient(far_side, label[near * CAP :])], axis=0
+    )
 
     d_new = iota((width, width), 0)
     d_old = iota((width, width), 1)
@@ -288,10 +325,7 @@
     bf16, f32 = jnp.bfloat16, jnp.float32
     return pl.pallas_call(
         functools.partial(step_kernel, owners, groups),
-        out_shape=(
-            jax.ShapeDtypeStruct((2, tokens), f32),
-            jax.ShapeDtypeStruct((1, part, expert), f32),
-        ),
+        out_shape=(pltpu.VMEM((2, tokens), f32), pltpu.VMEM((1, part, expert), f32)),
         in_specs=[vmem, vmem, vmem, pl.BlockSpec(memory_space=pltpu.SMEM), hbm, hbm, vmem, hbm, vmem],
         out_specs=(vmem, vmem),
         scratch_shapes=[
@@ -318,6 +352,7 @@
             dma(()),
             dma(()),
             dma(()),
+            pltpu.SemaphoreType.REGULAR,
             dma((CHUNKS,)),
             dma((CHUNKS,)),
             dma((CHUNKS, chips - 1)),
@@ -331,9 +366,9 @@
         counts,
         scenario_weights,
         shared_weights,
-        gate_weights,
+        gate_weights.T,
         tower_weights,
-        tower_out.reshape(1, towers),
+        tower_out.reshape(2, towers // 2),
     )
 
 

time: 55.1 us -> 47.8 us (0.87)
  local copies, waits for them, and re-layouts: 5.52 us -> 1.28 us
  Pallas kernels: 48.7 us -> 45.7 us
    unnamed x3 -> x2, local copies, waits for them, and re-layouts: 4.3 us -> 1.28 us
    pallas_call x1, Pallas kernels: 48.7 us -> 45.7 us  [shards(): pl.pallas_call(functools.partial(step_kernel, owners, groups), out_shape=...]
    reshape x1 -> x0, local copies, waits for them, and re-layouts: 1.22 us -> none  [shards(): tower_out.reshape(1, towers)]
where the time goes in v2:
time: 47.8 us; the launch traced here: 47.6 us
  Pallas kernels  45.7 us (96%)
  local copies, waits for them, and re-layouts  1.28 us (3%)
  between operations  0.64 us (1%)
    pallas_call x1, Pallas kernels, shards(): pl.pallas_call(functools.partial(step_kernel, owners, groups), out_shape=...  45.7 us
    unnamed x2, local copies, waits for them, and re-layouts  1.28 us

profile of v2, /device:TPU:1, one launch (start us, length us, event | category | flops | bytes accessed | tf_op | source)
XLA Modules:
  0.0 47.6 jit_solution(7957236312557087013)
XLA Ops:
  0.6 45.7 %shard_map.104 = (f32[2,256]{1,0:T(2,128)S(1)}, f32[1,16,4096]{2,1,0:T(8,128)S(1)}) custom-call(s32[1,256]{1,0:T(1,128)} %bitcast.3, s32[2,256]{1,0:T(2,128)} %labels_ref.1, bf16[256,128]{1,0:T(8,128)(2,1)} %feats_ref.1, s32[64]{0:T(128)} %counts_ref.1, bf16[1,128,4096]{2,1,0:T(8,128)(2,1)} %w_hbm.1, bf16[128,4096]{1,0:T(8,128)(2,1)} %s_hbm.1, ...), custom_call_target="tpu_custom_call" | custom-call | tf_op jit(solution)/shard_map/pallas_call | solution.py:326
  46.3 0.6 %copy.13 = f32[2,256]{1,0:T(2,128)} copy(f32[2,256]{1,0:T(2,128)S(1)} %get-tuple-element.2) | data formatting | bytes 4096
  46.9 0.7 %copy.14 = f32[1,16,4096]{2,1,0:T(8,128)} copy(f32[1,16,4096]{2,1,0:T(8,128)S(1)} %get-tuple-element.3) | data formatting | bytes 524288

commit v3 on v2

--- a/solution.py
+++ b/solution.py
@@ -53,6 +53,8 @@
     core_f,
     link_s,
     link_r,
+    sum_s,
+    sum_r,
     load_sem,
     x_send,
     x_recv,
@@ -65,6 +67,8 @@
     core_recv,
     link_send,
     link_recv,
+    sum_send,
+    sum_recv,
 ):
     own = lax.axis_index("own")
     grp = lax.axis_index("grp")
@@ -150,12 +154,12 @@
 
         return body
 
-    def send_label(offset):
+    def send_label(offset, group):
         def body(i, carry):
             off = offset(i)
             spot = spot_of(off)
             pltpu.make_async_remote_copy(
-                lab_s.at[spot], lab_r.at[spot], lab_send, lab_recv, device_id=(grp, ahead(off)), device_id_type=MESH
+                lab_s.at[spot], lab_r.at[spot], lab_send, lab_recv.at[group], device_id=(grp, ahead(off)), device_id_type=MESH
             ).start()
             return carry
 
@@ -165,10 +169,10 @@
     for end in (REACH, zs - REACH):
         pl.semaphore_signal(near_sem, inc=1, device_id=(grp, lax.rem(z + end, zs) * YS + y), device_id_type=MESH)
     lax.fori_loop(0, near - 1, send_x(near_offset, 0), 0)
+    lax.fori_loop(0, near - 1, send_label(near_offset, 0), 0)
     pl.semaphore_wait(near_sem, 2)
     lax.fori_loop(0, far, send_x(far_offset, 1), 0)
-    lax.fori_loop(0, near - 1, send_label(near_offset), 0)
-    lax.fori_loop(0, far, send_label(far_offset), 0)
+    lax.fori_loop(0, far, send_label(far_offset, 1), 0)
     x_ref[turn] = out_x[turn]
     lab_r[turn] = lab_s[turn]
 
@@ -225,78 +229,94 @@
 
         return body
 
+    fan = (lax.rem(iota((LANES, 2 * LANES), 0), 2) == lax.div(iota((LANES, 2 * LANES), 1), LANES)).astype(jnp.float32).astype(jnp.bfloat16)
+    weight = 64.0 / jnp.sqrt(jnp.full((1, 2 * LANES), counts_ref[own], jnp.int32).astype(jnp.float32))
+    d_new = iota((width, width), 0)
+    d_old = iota((width, width), 1)
+    from_row = (2 * lax.rem(lax.div(d_new, part), chips) + lax.div(d_new, part * chips)) * part + lax.rem(d_new, part)
+    order = (d_old == from_row).astype(jnp.float32).astype(jnp.bfloat16)
+
+    def gradient(first, blocks, side):
+        gate, tower_in, logit = side
+        block = blocks * CAP
+        spread = (lax.div(iota((block, blocks), 0), CAP) == iota((block, blocks), 1)).astype(jnp.float32).astype(jnp.bfloat16)
+        packed = dot(spread, lab_r[pl.ds(first, blocks)].reshape(blocks, LANES).astype(jnp.bfloat16))
+        packed = jnp.where(own_lane(blocks)[1], packed, 0.0).astype(jnp.bfloat16)
+        dlogit = weight * (jax.nn.sigmoid(logit) - dot(packed, fan))
+        mixed = jnp.where(tower_in > 0.0, gate * dlogit * tout, 0.0).astype(jnp.bfloat16)
+        x = x_ref[pl.ds(first, blocks)].reshape(block, width)
+        return mixed, dot(order, x, ((1,), (1,))).astype(jnp.bfloat16)
+
+    def share(first, blocks, mixed, x_t, c):
+        at = pl.ds(c * cols, cols)
+        back = dot(mixed, t_ref[at, :], ((1,), (1,))).astype(jnp.bfloat16)
+        masked = jnp.where(hidden[pl.ds(first * CAP, blocks * CAP), at] > 0.0, back, jnp.zeros_like(back))
+        return dot(x_t, masked).reshape(2, width // 2, cols)
+
+    def core_copy(c):
+        return pltpu.make_async_remote_copy(
+            core_s.at[c, 1 - core], core_r.at[c], core_send.at[c], core_recv.at[c], device_id=partner, device_id_type=MESH
+        )
+
+    def link_copy(src, dst, send, recv, c, way):
+        to = lax.rem(chip + (1, chips - 1)[way], chips)
+        return pltpu.make_async_remote_copy(
+            src.at[c, way],
+            dst.at[c, way],
+            send.at[c, way],
+            recv.at[c, way],
+            device_id=(2 * to + core, own),
+            device_id_type=MESH,
+        )
+
+    def first_leg(c, way):
+        return link_copy(link_s, link_r, link_send, link_recv, c, way)
+
+    def second_leg(c, way):
+        return link_copy(sum_s, sum_r, sum_send, sum_recv, c, way)
+
     bulk(out_x, x_ref, near - 1, x_send, x_recv.at[0]).wait_recv()
     near_side = forward(0, near)
     lax.fori_loop(0, near - 1, send_logit(near_offset), 0)
     lg_r[turn] = lg_s[turn]
+    bulk(lab_s, lab_r, near - 1, lab_send, lab_recv.at[0]).wait_recv()
+    mixed, x_t = gradient(0, near, near_side)
+    for c in range(CHUNKS):
+        core_f[c] = share(0, near, mixed, x_t, c)
     bulk(out_x, x_ref, far, x_send, x_recv.at[1]).wait_recv()
     far_side = forward(near, far)
     lax.fori_loop(0, far, send_logit(far_offset), 0)
-
-    bulk(lab_s, lab_r, owners - 1, lab_send, lab_recv).wait_recv()
-    spread = (lax.div(iota((rows, owners), 0), CAP) == iota((rows, owners), 1)).astype(jnp.float32).astype(jnp.bfloat16)
-    packed = dot(spread, lab_r[...].reshape(owners, LANES).astype(jnp.bfloat16))
-    packed = jnp.where(own_lane(owners)[1], packed, 0.0).astype(jnp.bfloat16)
-    fan = (lax.rem(iota((LANES, 2 * LANES), 0), 2) == lax.div(iota((LANES, 2 * LANES), 1), LANES)).astype(jnp.float32).astype(jnp.bfloat16)
-    label = dot(packed, fan)
-    weight = 64.0 / jnp.sqrt(jnp.full((1, 2 * LANES), counts_ref[own], jnp.int32).astype(jnp.float32))
-
-    def gradient(side, label):
-        gate, tower_in, logit = side
-        dlogit = weight * (jax.nn.sigmoid(logit) - label)
-        return jnp.where(tower_in > 0.0, gate * dlogit * tout, 0.0).astype(jnp.bfloat16)
-
-    mixed = jnp.concatenate(
-        [gradient(near_side, label[: near * CAP]), gradient(far_side, label[near * CAP :])], axis=0
-    )
-
-    d_new = iota((width, width), 0)
-    d_old = iota((width, width), 1)
-    from_row = (2 * lax.rem(lax.div(d_new, part), chips) + lax.div(d_new, part * chips)) * part + lax.rem(d_new, part)
-    order = (d_old == from_row).astype(jnp.float32).astype(jnp.bfloat16)
-    x_t = dot(order, x_ref[...].reshape(rows, width), ((1,), (1,))).astype(jnp.bfloat16)
-
-    def core_copy(c):
-        return pltpu.make_async_remote_copy(
-            core_s.at[c, 1 - core], core_r.at[c], core_send.at[c], core_recv.at[c], device_id=partner, device_id_type=MESH
-        )
-
-    def link_copy(c, d):
-        to = lax.rem(chip + d, chips)
-        return pltpu.make_async_remote_copy(
-            link_s.at[c, to],
-            link_r.at[c, d - 1],
-            link_send.at[c, d - 1],
-            link_recv.at[c, d - 1],
-            device_id=(2 * to + core, own),
-            device_id_type=MESH,
-        )
-
-    def relay(c):
+    bulk(lab_s, lab_r, far, lab_send, lab_recv.at[1]).wait_recv()
+    mixed, x_t = gradient(near, far, far_side)
+    for c in range(CHUNKS):
+        total = core_f[c] + share(near, far, mixed, x_t, c)
+        core_f[c] = total
+        core_s[c] = total.astype(jnp.bfloat16)
+        core_copy(c).start()
+
+    after, opposite, prior = (lax.rem(chip + d, chips) for d in (1, 2, 3))
+    side = cols // 2
+    for c in range(CHUNKS):
         core_copy(c).wait_recv()
-        total = core_f[c, core] + core_r[c].astype(jnp.float32)
-        proj[c] = total.reshape(chips, part, cols)
-        link_s[c] = total.astype(jnp.bfloat16).reshape(chips, part, cols)
-        for d in (2, 1, 3):
-            link_copy(c, d).start()
-
-    for c in range(CHUNKS):
-        at = pl.ds(c * cols, cols)
-        back = dot(mixed, t_ref[at, :], ((1,), (1,))).astype(jnp.bfloat16)
-        masked = jnp.where(hidden[:, at] > 0.0, back, jnp.zeros_like(back))
-        share = dot(x_t, masked)
-        core_f[c] = share.reshape(2, width // 2, cols)
-        core_s[c] = share.astype(jnp.bfloat16).reshape(2, width // 2, cols)
-        core_copy(c).start()
-        if c > 0:
-            relay(c - 1)
-    relay(CHUNKS - 1)
-    for c in range(CHUNKS):
-        total = proj[c, chip]
-        for d in range(1, chips):
-            link_copy(c, d).wait_recv()
-            total = total + link_r[c, d - 1].astype(jnp.float32)
-        grad_ref[0, :, pl.ds(c * cols, cols)] = total
+        proj[c] = (core_f[c, core] + core_r[c].astype(jnp.float32)).reshape(chips, part, cols)
+        link_s[c, 0, 0] = proj[c, opposite, :, pl.ds(0, side)].astype(jnp.bfloat16)
+        link_s[c, 0, 1] = proj[c, after, :, pl.ds(side, side)].astype(jnp.bfloat16)
+        first_leg(c, 0).start()
+        link_s[c, 1, 0] = proj[c, opposite, :, pl.ds(side, side)].astype(jnp.bfloat16)
+        link_s[c, 1, 1] = proj[c, prior, :, pl.ds(0, side)].astype(jnp.bfloat16)
+        first_leg(c, 1).start()
+    for c in range(CHUNKS):
+        first_leg(c, 0).wait_recv()
+        sum_s[c, 0] = (proj[c, after, :, pl.ds(0, side)] + link_r[c, 0, 0].astype(jnp.float32)).astype(jnp.bfloat16)
+        second_leg(c, 0).start()
+        first_leg(c, 1).wait_recv()
+        sum_s[c, 1] = (proj[c, prior, :, pl.ds(side, side)] + link_r[c, 1, 0].astype(jnp.float32)).astype(jnp.bfloat16)
+        second_leg(c, 1).start()
+    for c in range(CHUNKS):
+        for way in range(2):
+            second_leg(c, way).wait_recv()
+            total = proj[c, chip, :, pl.ds(way * side, side)] + link_r[c, 1 - way, 1].astype(jnp.float32)
+            grad_ref[0, :, pl.ds(c * cols + way * side, side)] = total + sum_r[c, way].astype(jnp.float32)
 
     bulk(lg_s, lg_r, owners - 1, lg_send, lg_recv).wait_recv()
     got = lg_r[...].reshape(owners, LANES)
@@ -305,12 +325,13 @@
         logits_ref[pl.ds(task, 1), :] = jnp.sum(jnp.where(lane_t == 2 * rank + task, found, 0.0), axis=0, keepdims=True)
 
     bulk(out_x, x_ref, owners - 1, x_send, x_recv.at[0]).wait_send()
-    bulk(lab_s, lab_r, owners - 1, lab_send, lab_recv).wait_send()
+    bulk(lab_s, lab_r, owners - 1, lab_send, lab_recv.at[0]).wait_send()
     bulk(lg_s, lg_r, owners - 1, lg_send, lg_recv).wait_send()
     for c in range(CHUNKS):
         core_copy(c).wait_send()
-        for d in range(1, chips):
-            link_copy(c, d).wait_send()
+        for way in range(2):
+            first_leg(c, way).wait_send()
+            second_leg(c, way).wait_send()
 
 
 def shards(owners, groups, features, scenario_ids, labels, counts, scenario_weights, shared_weights, gate_weights, tower_weights, tower_out):
@@ -343,20 +364,24 @@
             pltpu.VMEM((CHUNKS, 2, width // 2, cols), bf16),
             pltpu.VMEM((CHUNKS, width // 2, cols), bf16),
             pltpu.VMEM((CHUNKS, 2, width // 2, cols), f32),
-            pltpu.VMEM((CHUNKS, chips, part, cols), bf16),
-            pltpu.VMEM((CHUNKS, chips - 1, part, cols), bf16),
+            pltpu.VMEM((CHUNKS, 2, 2, part, cols // 2), bf16),
+            pltpu.VMEM((CHUNKS, 2, 2, part, cols // 2), bf16),
+            pltpu.VMEM((CHUNKS, 2, part, cols // 2), bf16),
+            pltpu.VMEM((CHUNKS, 2, part, cols // 2), bf16),
             dma((3,)),
             dma(()),
             dma((2,)),
             dma(()),
-            dma(()),
+            dma((2,)),
             dma(()),
             dma(()),
             pltpu.SemaphoreType.REGULAR,
             dma((CHUNKS,)),
             dma((CHUNKS,)),
-            dma((CHUNKS, chips - 1)),
-            dma((CHUNKS, chips - 1)),
+            dma((CHUNKS, 2)),
+            dma((CHUNKS, 2)),
+            dma((CHUNKS, 2)),
+            dma((CHUNKS, 2)),
         ],
         compiler_params=pltpu.CompilerParams(collective_id=0, has_side_effects=True, vmem_limit_bytes=56 * 1024 * 1024),
     )(

time: 47.8 us -> 46.1 us (0.964)
  Pallas kernels: 45.7 us -> 43.6 us
    pallas_call x1, Pallas kernels: 45.7 us -> 43.6 us  [shards(): pl.pallas_call(functools.partial(step_kernel, owners, groups), out_shape=...]
where the time goes in v3:
time: 46.1 us; the launch traced here: 45.6 us
  Pallas kernels  43.6 us (95%)
  local copies, waits for them, and re-layouts  1.28 us (3%)
  between operations  0.64 us (1%)
    pallas_call x1, Pallas kernels, shards(): pl.pallas_call(functools.partial(step_kernel, owners, groups), out_shape=...  43.6 us
    unnamed x2, local copies, waits for them, and re-layouts  1.28 us

profile of v3, /device:TPU:1, one launch (start us, length us, event | category | flops | bytes accessed | tf_op | source)
XLA Modules:
  0.0 45.6 jit_solution(3098441412607146671)
XLA Ops:
  0.6 43.6 %shard_map.104 = (f32[2,256]{1,0:T(2,128)S(1)}, f32[1,16,4096]{2,1,0:T(8,128)S(1)}) custom-call(s32[1,256]{1,0:T(1,128)} %bitcast.3, s32[2,256]{1,0:T(2,128)} %labels_ref.1, bf16[256,128]{1,0:T(8,128)(2,1)} %feats_ref.1, s32[64]{0:T(128)} %counts_ref.1, bf16[1,128,4096]{2,1,0:T(8,128)(2,1)} %w_hbm.1, bf16[128,4096]{1,0:T(8,128)(2,1)} %s_hbm.1, ...), custom_call_target="tpu_custom_call" | custom-call | tf_op jit(solution)/shard_map/pallas_call | solution.py:347
  44.3 0.6 %copy.13 = f32[2,256]{1,0:T(2,128)} copy(f32[2,256]{1,0:T(2,128)S(1)} %get-tuple-element.2) | data formatting | bytes 4096
  44.9 0.7 %copy.14 = f32[1,16,4096]{2,1,0:T(8,128)} copy(f32[1,16,4096]{2,1,0:T(8,128)S(1)} %get-tuple-element.3) | data formatting | bytes 524288

commit v4 on v3

--- a/solution.py
+++ b/solution.py
@@ -26,17 +26,23 @@
 def step_kernel(
     owners,
     groups,
+    ids_hbm,
+    labels_hbm,
+    feats_hbm,
+    counts_hbm,
+    w_hbm,
+    s_hbm,
+    gate_hbm,
+    t_hbm,
+    tout_hbm,
+    logits_ref,
+    grad_ref,
     ids_ref,
     labels_ref,
     feats_ref,
     counts_ref,
-    w_hbm,
-    s_hbm,
     gate_ref,
-    t_hbm,
     tout_ref,
-    logits_ref,
-    grad_ref,
     w_ref,
     s_ref,
     t_ref,
@@ -82,7 +88,7 @@
     turn = REACH * YS
     near = 2 * turn + YS
     far = owners - near
-    tokens, width = feats_ref.shape
+    tokens, width = feats_hbm.shape
     expert = w_ref.shape[1]
     cols = expert // CHUNKS
     rows = owners * CAP
@@ -121,9 +127,19 @@
         pltpu.make_async_copy(w_hbm.at[0], w_ref, load_sem.at[0]),
         pltpu.make_async_copy(s_hbm, s_ref, load_sem.at[1]),
         pltpu.make_async_copy(t_hbm, t_ref, load_sem.at[2]),
+        pltpu.make_async_copy(counts_hbm, counts_ref, load_sem.at[3]),
+        pltpu.make_async_copy(gate_hbm, gate_ref, load_sem.at[4]),
+        pltpu.make_async_copy(tout_hbm, tout_ref, load_sem.at[5]),
     ]
-    for load in loads:
+    firsts = [
+        pltpu.make_async_copy(ids_hbm, ids_ref, load_sem.at[6]),
+        pltpu.make_async_copy(labels_hbm, labels_ref, load_sem.at[7]),
+        pltpu.make_async_copy(feats_hbm, feats_ref, load_sem.at[8]),
+    ]
+    for load in firsts + loads:
         load.start()
+    for load in firsts:
+        load.wait()
 
     ids = ids_ref[...]
     to_z = lax.rem(lax.div(ids, YS) - z + zs, zs)
@@ -285,7 +301,6 @@
         core_f[c] = share(0, near, mixed, x_t, c)
     bulk(out_x, x_ref, far, x_send, x_recv.at[1]).wait_recv()
     far_side = forward(near, far)
-    lax.fori_loop(0, far, send_logit(far_offset), 0)
     bulk(lab_s, lab_r, far, lab_send, lab_recv.at[1]).wait_recv()
     mixed, x_t = gradient(near, far, far_side)
     for c in range(CHUNKS):
@@ -293,6 +308,7 @@
         core_f[c] = total
         core_s[c] = total.astype(jnp.bfloat16)
         core_copy(c).start()
+    lax.fori_loop(0, far, send_logit(far_offset), 0)
 
     after, opposite, prior = (lax.rem(chip + d, chips) for d in (1, 2, 3))
     side = cols // 2
@@ -312,17 +328,17 @@
         first_leg(c, 1).wait_recv()
         sum_s[c, 1] = (proj[c, prior, :, pl.ds(side, side)] + link_r[c, 1, 0].astype(jnp.float32)).astype(jnp.bfloat16)
         second_leg(c, 1).start()
-    for c in range(CHUNKS):
-        for way in range(2):
-            second_leg(c, way).wait_recv()
-            total = proj[c, chip, :, pl.ds(way * side, side)] + link_r[c, 1 - way, 1].astype(jnp.float32)
-            grad_ref[0, :, pl.ds(c * cols + way * side, side)] = total + sum_r[c, way].astype(jnp.float32)
-
     bulk(lg_s, lg_r, owners - 1, lg_send, lg_recv).wait_recv()
     got = lg_r[...].reshape(owners, LANES)
     found = dot(got, member.astype(jnp.float32), ((0,), (0,)), lax.Precision.HIGHEST)
     for task in range(2):
         logits_ref[pl.ds(task, 1), :] = jnp.sum(jnp.where(lane_t == 2 * rank + task, found, 0.0), axis=0, keepdims=True)
+
+    for c in range(CHUNKS):
+        for way in range(2):
+            second_leg(c, way).wait_recv()
+            total = proj[c, chip, :, pl.ds(way * side, side)] + link_r[c, 1 - way, 1].astype(jnp.float32)
+            grad_ref[0, :, pl.ds(c * cols + way * side, side)] = total + sum_r[c, way].astype(jnp.float32)
 
     bulk(out_x, x_ref, owners - 1, x_send, x_recv.at[0]).wait_send()
     bulk(lab_s, lab_r, owners - 1, lab_send, lab_recv.at[0]).wait_send()
@@ -341,15 +357,21 @@
     part = width // groups
     chips = groups // 2
     vmem = pl.BlockSpec(memory_space=pltpu.VMEM)
-    hbm = pl.BlockSpec(memory_space=pl.ANY)
+    hbm = pl.BlockSpec(memory_space=pltpu.HBM)
     dma = pltpu.SemaphoreType.DMA
     bf16, f32 = jnp.bfloat16, jnp.float32
     return pl.pallas_call(
         functools.partial(step_kernel, owners, groups),
         out_shape=(pltpu.VMEM((2, tokens), f32), pltpu.VMEM((1, part, expert), f32)),
-        in_specs=[vmem, vmem, vmem, pl.BlockSpec(memory_space=pltpu.SMEM), hbm, hbm, vmem, hbm, vmem],
+        in_specs=[hbm] * 9,
         out_specs=(vmem, vmem),
         scratch_shapes=[
+            pltpu.VMEM((1, tokens), jnp.int32),
+            pltpu.VMEM((2, tokens), jnp.int32),
+            pltpu.VMEM((tokens, width), bf16),
+            pltpu.SMEM((owners,), jnp.int32),
+            pltpu.VMEM((2, width), bf16),
+            pltpu.VMEM((2, towers // 2), bf16),
             pltpu.VMEM((width, expert), bf16),
             pltpu.VMEM((width, expert), bf16),
             pltpu.VMEM((expert, towers), bf16),
@@ -368,7 +390,7 @@
             pltpu.VMEM((CHUNKS, 2, 2, part, cols // 2), bf16),
             pltpu.VMEM((CHUNKS, 2, part, cols // 2), bf16),
             pltpu.VMEM((CHUNKS, 2, part, cols // 2), bf16),
-            dma((3,)),
+            dma((9,)),
             dma(()),
             dma((2,)),
             dma(()),

time: 46.1 us -> 44.6 us (0.967)
  Pallas kernels: 43.6 us -> 41.8 us
    pallas_call x1, Pallas kernels: 43.6 us -> 41.8 us  [shards(): pl.pallas_call(functools.partial(step_kernel, owners, groups), out_shape=...]
where the time goes in v4:
time: 44.6 us; the launch traced here: 43.8 us
  Pallas kernels  41.8 us (94%)
  local copies, waits for them, and re-layouts  1.28 us (3%)
  between operations  0.64 us (1%)
    pallas_call x1, Pallas kernels, shards(): pl.pallas_call(functools.partial(step_kernel, owners, groups), out_shape=...  41.8 us
    unnamed x2, local copies, waits for them, and re-layouts  1.28 us

profile of v4, /device:TPU:1, one launch (start us, length us, event | category | flops | bytes accessed | tf_op | source)
XLA Modules:
  0.0 43.8 jit_solution(13554648527337060267)
XLA Ops:
  0.6 41.8 %shard_map.104 = (f32[2,256]{1,0:T(2,128)S(1)}, f32[1,16,4096]{2,1,0:T(8,128)S(1)}) custom-call(s32[1,256]{1,0:T(1,128)} %bitcast.3, s32[2,256]{1,0:T(2,128)} %labels_hbm.1, bf16[256,128]{1,0:T(8,128)(2,1)} %feats_hbm.1, s32[64]{0:T(128)} %counts_hbm.1, bf16[1,128,4096]{2,1,0:T(8,128)(2,1)} %w_hbm.1, bf16[128,4096]{1,0:T(8,128)(2,1)} %s_hbm.1, ...), custom_call_target="tpu_custom_call" | custom-call | tf_op jit(solution)/shard_map/pallas_call | solution.py:363
  42.5 0.6 %copy.13 = f32[2,256]{1,0:T(2,128)} copy(f32[2,256]{1,0:T(2,128)S(1)} %get-tuple-element.2) | data formatting | bytes 4096
  43.1 0.7 %copy.14 = f32[1,16,4096]{2,1,0:T(8,128)} copy(f32[1,16,4096]{2,1,0:T(8,128)S(1)} %get-tuple-element.3) | data formatting | bytes 524288

commit v5 on v4

--- a/solution.py
+++ b/solution.py
@@ -114,11 +114,21 @@
     def behind(off):
         return lax.rem(z + zs - lax.div(off, YS), zs) * YS + lax.rem(y + YS - lax.rem(off, YS), YS)
 
-    def greet(i, carry):
-        pl.semaphore_signal(barrier, inc=1, device_id=(grp, ahead(near_offset(i))), device_id_type=MESH)
-        return carry
-
-    lax.fori_loop(0, near - 1, greet, 0)
+    early_z = zs // 2
+    early = z < early_z
+
+    def greet(offset):
+        def body(i, carry):
+            pl.semaphore_signal(barrier, inc=1, device_id=(grp, ahead(offset(i))), device_id_type=MESH)
+            return carry
+
+        return body
+
+    @pl.when(early)
+    def _():
+        lax.fori_loop(0, far, greet(far_offset), 0)
+
+    lax.fori_loop(0, near - 1, greet(near_offset), 0)
     pl.semaphore_signal(barrier, inc=1, device_id=partner, device_id_type=MESH)
     for d in range(1, chips):
         pl.semaphore_signal(barrier, inc=1, device_id=(lax.rem(grp + 2 * d, groups), own), device_id_type=MESH)
@@ -181,13 +191,30 @@
 
         return body
 
-    pl.semaphore_wait(barrier, near - 1 + 1 + chips - 1)
+    def send_far(to_early):
+        def body(i, carry):
+            dest = lax.rem(z + lax.div(far_offset(i), YS), zs)
+
+            @pl.when((dest < early_z) if to_early else (dest >= early_z))
+            def _():
+                send_x(far_offset, 1)(i, 0)
+
+            return carry
+
+        return body
+
+    greeted = early_z * YS - jnp.where(early, 1, 0) + jnp.where(early, 0, YS - 1)
+    for d in range(1, REACH + 1):
+        for end in (d, zs - d):
+            greeted = greeted + jnp.where(lax.rem(z + end, zs) < early_z, 0, YS)
+    pl.semaphore_wait(barrier, greeted + 1 + chips - 1)
     for end in (REACH, zs - REACH):
         pl.semaphore_signal(near_sem, inc=1, device_id=(grp, lax.rem(z + end, zs) * YS + y), device_id_type=MESH)
+    lax.fori_loop(0, far, send_far(True), 0)
     lax.fori_loop(0, near - 1, send_x(near_offset, 0), 0)
     lax.fori_loop(0, near - 1, send_label(near_offset, 0), 0)
     pl.semaphore_wait(near_sem, 2)
-    lax.fori_loop(0, far, send_x(far_offset, 1), 0)
+    lax.fori_loop(0, far, send_far(False), 0)
     lax.fori_loop(0, far, send_label(far_offset, 1), 0)
     x_ref[turn] = out_x[turn]
     lab_r[turn] = lab_s[turn]
@@ -301,6 +328,11 @@
         core_f[c] = share(0, near, mixed, x_t, c)
     bulk(out_x, x_ref, far, x_send, x_recv.at[1]).wait_recv()
     far_side = forward(near, far)
+
+    @pl.when(z >= early_z)
+    def _():
+        lax.fori_loop(0, far, send_logit(far_offset), 0)
+
     bulk(lab_s, lab_r, far, lab_send, lab_recv.at[1]).wait_recv()
     mixed, x_t = gradient(near, far, far_side)
     for c in range(CHUNKS):
@@ -308,7 +340,10 @@
         core_f[c] = total
         core_s[c] = total.astype(jnp.bfloat16)
         core_copy(c).start()
-    lax.fori_loop(0, far, send_logit(far_offset), 0)
+
+    @pl.when(early)
+    def _():
+        lax.fori_loop(0, far, send_logit(far_offset), 0)
 
     after, opposite, prior = (lax.rem(chip + d, chips) for d in (1, 2, 3))
     side = cols // 2

time: 44.6 us -> 48.8 us (1.094)
  the two profiles are of different devices: /device:TPU:1 before, /device:TPU:2 now
where the time goes in v5:
time: 48.8 us; the launch traced here: 48.7 us
  Pallas kernels  46.8 us (96%)
  local copies, waits for them, and re-layouts  1.28 us (3%)
  between operations  0.64 us (1%)
    pallas_call x1, Pallas kernels, shards(): pl.pallas_call(functools.partial(step_kernel, owners, groups), out_shape=...  46.8 us
    unnamed x2, local copies, waits for them, and re-layouts  1.28 us

profile of v5, /device:TPU:2, one launch (start us, length us, event | category | flops | bytes accessed | tf_op | source)
XLA Modules:
  0.0 48.7 jit_solution(5278281734349971151)
XLA Ops:
  0.6 46.8 %shard_map.104 = (f32[2,256]{1,0:T(2,128)S(1)}, f32[1,16,4096]{2,1,0:T(8,128)S(1)}) custom-call(s32[1,256]{1,0:T(1,128)} %bitcast.3, s32[2,256]{1,0:T(2,128)} %labels_hbm.1, bf16[256,128]{1,0:T(8,128)(2,1)} %feats_hbm.1, s32[64]{0:T(128)} %counts_hbm.1, bf16[1,128,4096]{2,1,0:T(8,128)(2,1)} %w_hbm.1, bf16[128,4096]{1,0:T(8,128)(2,1)} %s_hbm.1, ...), custom_call_target="tpu_custom_call" | custom-call | tf_op jit(solution)/shard_map/pallas_call | solution.py:398
  47.4 0.6 %copy.13 = f32[2,256]{1,0:T(2,128)} copy(f32[2,256]{1,0:T(2,128)S(1)} %get-tuple-element.2) | data formatting | bytes 4096
  48.0 0.7 %copy.14 = f32[1,16,4096]{2,1,0:T(8,128)} copy(f32[1,16,4096]{2,1,0:T(8,128)S(1)} %get-tuple-element.3) | data formatting | bytes 524288

commit v6 on v4

--- a/solution.py
+++ b/solution.py
@@ -59,8 +59,6 @@
     core_f,
     link_s,
     link_r,
-    sum_s,
-    sum_r,
     load_sem,
     x_send,
     x_recv,
@@ -73,8 +71,6 @@
     core_recv,
     link_send,
     link_recv,
-    sum_send,
-    sum_recv,
 ):
     own = lax.axis_index("own")
     grp = lax.axis_index("grp")
@@ -96,29 +92,44 @@
 
     barrier = pltpu.get_barrier_semaphore()
 
-    def near_offset(i):
-        k = lax.div(i, 2)
-        off = jnp.where(lax.rem(i, 2) == 0, turn + YS - 1 - k, owners - turn + k)
-        return jnp.where(off == owners, 1, off)
-
-    def far_offset(i):
-        k = lax.div(i, 2)
-        return jnp.where(lax.rem(i, 2) == 0, turn + YS + far // 2 - 1 - k, turn + YS + far // 2 + k)
-
-    def spot_of(off):
-        return lax.rem(off + turn, owners)
-
-    def ahead(off):
-        return lax.rem(z + lax.div(off, YS), zs) * YS + lax.rem(y + lax.rem(off, YS), YS)
-
-    def behind(off):
-        return lax.rem(z + zs - lax.div(off, YS), zs) * YS + lax.rem(y + YS - lax.rem(off, YS), YS)
-
-    def greet(i, carry):
-        pl.semaphore_signal(barrier, inc=1, device_id=(grp, ahead(near_offset(i))), device_id_type=MESH)
-        return carry
-
-    lax.fori_loop(0, near - 1, greet, 0)
+    def wrap(v, n):
+        return jnp.where(v < 0, v + n, jnp.where(v >= n, v - n, v))
+
+    y_ahead = [wrap(y + d, YS) for d in range(YS)]
+    y_behind = [wrap(y - d, YS) for d in range(YS)]
+
+    def row(send, v, first=0, back=False):
+        to_z = wrap(z - v if back else z + v, zs) * YS
+        for d in range(first, YS):
+            send(turn + YS * v + d, to_z + (y_behind if back else y_ahead)[d])
+
+    def near_rows(send, back=False):
+        def body(i, carry):
+            row(send, REACH - i, back=back)
+            row(send, i - REACH, back=back)
+            return carry
+
+        lax.fori_loop(0, REACH, body, 0)
+        row(send, 0, 1, back)
+
+    def far_rows(send, back=False):
+        def one(v):
+            row(send, v, back=back)
+
+        def body(i, carry):
+            one(zs // 2 - i)
+            one(zs // 2 + i)
+            return carry
+
+        one(zs // 2)
+        lax.fori_loop(1, zs // 2 - REACH, body, 0)
+
+    def greet(spot, target):
+        pl.semaphore_signal(barrier, inc=1, device_id=(grp, target), device_id_type=MESH)
+
+    early_z = zs // 2
+    early = z < early_z
+    near_rows(greet)
     pl.semaphore_signal(barrier, inc=1, device_id=partner, device_id_type=MESH)
     for d in range(1, chips):
         pl.semaphore_signal(barrier, inc=1, device_id=(lax.rem(grp + 2 * d, groups), own), device_id_type=MESH)
@@ -144,7 +155,7 @@
     ids = ids_ref[...]
     to_z = lax.rem(lax.div(ids, YS) - z + zs, zs)
     to_y = lax.rem(lax.rem(ids, YS) - y + YS, YS)
-    spots = spot_of(to_z * YS + to_y)
+    spots = lax.rem(to_z * YS + to_y + turn, owners)
     member = iota((owners, tokens), 0) == spots
     member_b = member.astype(jnp.float32).astype(jnp.bfloat16)
     before = (iota((tokens, tokens), 0) < iota((tokens, tokens), 1)).astype(jnp.float32).astype(jnp.bfloat16)
@@ -159,36 +170,31 @@
     label_at = jnp.where(lax.div(lane_t, 2) == rank, label_of, 0.0).astype(jnp.bfloat16)
     lab_s[...] = dot(member_b, label_at, ((1,), (1,))).reshape(owners, 1, LANES)
 
-    def send_x(offset, group):
-        def body(i, carry):
-            off = offset(i)
-            spot = spot_of(off)
+    def send_x(group):
+        def send(spot, target):
             pltpu.make_async_remote_copy(
-                out_x.at[spot], x_ref.at[spot], x_send, x_recv.at[group], device_id=(grp, ahead(off)), device_id_type=MESH
+                out_x.at[spot], x_ref.at[spot], x_send, x_recv.at[group], device_id=(grp, target), device_id_type=MESH
             ).start()
-            return carry
-
-        return body
-
-    def send_label(offset, group):
-        def body(i, carry):
-            off = offset(i)
-            spot = spot_of(off)
+
+        return send
+
+    def send_label(group):
+        def send(spot, target):
             pltpu.make_async_remote_copy(
-                lab_s.at[spot], lab_r.at[spot], lab_send, lab_recv.at[group], device_id=(grp, ahead(off)), device_id_type=MESH
+                lab_s.at[spot], lab_r.at[spot], lab_send, lab_recv.at[group], device_id=(grp, target), device_id_type=MESH
             ).start()
-            return carry
-
-        return body
-
-    pl.semaphore_wait(barrier, near - 1 + 1 + chips - 1)
+
+        return send
+
+    greeted = near - 1
+    pl.semaphore_wait(barrier, greeted + 1 + chips - 1)
     for end in (REACH, zs - REACH):
         pl.semaphore_signal(near_sem, inc=1, device_id=(grp, lax.rem(z + end, zs) * YS + y), device_id_type=MESH)
-    lax.fori_loop(0, near - 1, send_x(near_offset, 0), 0)
-    lax.fori_loop(0, near - 1, send_label(near_offset, 0), 0)
+    near_rows(send_x(0))
+    near_rows(send_label(0))
     pl.semaphore_wait(near_sem, 2)
-    lax.fori_loop(0, far, send_x(far_offset, 1), 0)
-    lax.fori_loop(0, far, send_label(far_offset, 1), 0)
+    far_rows(send_x(1))
+    far_rows(send_label(1))
     x_ref[turn] = out_x[turn]
     lab_r[turn] = lab_s[turn]
 
@@ -234,16 +240,10 @@
         )
         return gate, tower_in, logit
 
-    def send_logit(offset):
-        def body(i, carry):
-            off = offset(i)
-            spot = spot_of(off)
-            pltpu.make_async_remote_copy(
-                lg_s.at[spot], lg_r.at[spot], lg_send, lg_recv, device_id=(grp, behind(off)), device_id_type=MESH
-            ).start()
-            return carry
-
-        return body
+    def send_logit(spot, target):
+        pltpu.make_async_remote_copy(
+            lg_s.at[spot], lg_r.at[spot], lg_send, lg_recv, device_id=(grp, target), device_id_type=MESH
+        ).start()
 
     fan = (lax.rem(iota((LANES, 2 * LANES), 0), 2) == lax.div(iota((LANES, 2 * LANES), 1), LANES)).astype(jnp.float32).astype(jnp.bfloat16)
     weight = 64.0 / jnp.sqrt(jnp.full((1, 2 * LANES), counts_ref[own], jnp.int32).astype(jnp.float32))
@@ -274,26 +274,20 @@
             core_s.at[c, 1 - core], core_r.at[c], core_send.at[c], core_recv.at[c], device_id=partner, device_id_type=MESH
         )
 
-    def link_copy(src, dst, send, recv, c, way):
-        to = lax.rem(chip + (1, chips - 1)[way], chips)
+    def link_copy(c, d):
+        to = lax.rem(chip + d, chips)
         return pltpu.make_async_remote_copy(
-            src.at[c, way],
-            dst.at[c, way],
-            send.at[c, way],
-            recv.at[c, way],
+            link_s.at[c, to],
+            link_r.at[c, d - 1],
+            link_send.at[c, d - 1],
+            link_recv.at[c, d - 1],
             device_id=(2 * to + core, own),
             device_id_type=MESH,
         )
 
-    def first_leg(c, way):
-        return link_copy(link_s, link_r, link_send, link_recv, c, way)
-
-    def second_leg(c, way):
-        return link_copy(sum_s, sum_r, sum_send, sum_recv, c, way)
-
     bulk(out_x, x_ref, near - 1, x_send, x_recv.at[0]).wait_recv()
     near_side = forward(0, near)
-    lax.fori_loop(0, near - 1, send_logit(near_offset), 0)
+    near_rows(send_logit, back=True)
     lg_r[turn] = lg_s[turn]
     bulk(lab_s, lab_r, near - 1, lab_send, lab_recv.at[0]).wait_recv()
     mixed, x_t = gradient(0, near, near_side)
@@ -301,6 +295,11 @@
         core_f[c] = share(0, near, mixed, x_t, c)
     bulk(out_x, x_ref, far, x_send, x_recv.at[1]).wait_recv()
     far_side = forward(near, far)
+
+    @pl.when(z >= early_z)
+    def _():
+        far_rows(send_logit, back=True)
+
     bulk(lab_s, lab_r, far, lab_send, lab_recv.at[1]).wait_recv()
     mixed, x_t = gradient(near, far, far_side)
     for c in range(CHUNKS):
@@ -308,26 +307,18 @@
         core_f[c] = total
         core_s[c] = total.astype(jnp.bfloat16)
         core_copy(c).start()
-    lax.fori_loop(0, far, send_logit(far_offset), 0)
-
-    after, opposite, prior = (lax.rem(chip + d, chips) for d in (1, 2, 3))
-    side = cols // 2
+
+    @pl.when(early)
+    def _():
+        far_rows(send_logit, back=True)
+
     for c in range(CHUNKS):
         core_copy(c).wait_recv()
-        proj[c] = (core_f[c, core] + core_r[c].astype(jnp.float32)).reshape(chips, part, cols)
-        link_s[c, 0, 0] = proj[c, opposite, :, pl.ds(0, side)].astype(jnp.bfloat16)
-        link_s[c, 0, 1] = proj[c, after, :, pl.ds(side, side)].astype(jnp.bfloat16)
-        first_leg(c, 0).start()
-        link_s[c, 1, 0] = proj[c, opposite, :, pl.ds(side, side)].astype(jnp.bfloat16)
-        link_s[c, 1, 1] = proj[c, prior, :, pl.ds(0, side)].astype(jnp.bfloat16)
-        first_leg(c, 1).start()
-    for c in range(CHUNKS):
-        first_leg(c, 0).wait_recv()
-        sum_s[c, 0] = (proj[c, after, :, pl.ds(0, side)] + link_r[c, 0, 0].astype(jnp.float32)).astype(jnp.bfloat16)
-        second_leg(c, 0).start()
-        first_leg(c, 1).wait_recv()
-        sum_s[c, 1] = (proj[c, prior, :, pl.ds(side, side)] + link_r[c, 1, 0].astype(jnp.float32)).astype(jnp.bfloat16)
-        second_leg(c, 1).start()
+        total = core_f[c, core] + core_r[c].astype(jnp.float32)
+        proj[c] = total.reshape(chips, part, cols)
+        link_s[c] = total.astype(jnp.bfloat16).reshape(chips, part, cols)
+        for d in (2, 1, 3):
+            link_copy(c, d).start()
     bulk(lg_s, lg_r, owners - 1, lg_send, lg_recv).wait_recv()
     got = lg_r[...].reshape(owners, LANES)
     found = dot(got, member.astype(jnp.float32), ((0,), (0,)), lax.Precision.HIGHEST)
@@ -335,19 +326,19 @@
         logits_ref[pl.ds(task, 1), :] = jnp.sum(jnp.where(lane_t == 2 * rank + task, found, 0.0), axis=0, keepdims=True)
 
     for c in range(CHUNKS):
-        for way in range(2):
-            second_leg(c, way).wait_recv()
-            total = proj[c, chip, :, pl.ds(way * side, side)] + link_r[c, 1 - way, 1].astype(jnp.float32)
-            grad_ref[0, :, pl.ds(c * cols + way * side, side)] = total + sum_r[c, way].astype(jnp.float32)
+        total = proj[c, chip]
+        for d in (1, 3, 2):
+            link_copy(c, d).wait_recv()
+            total = total + link_r[c, d - 1].astype(jnp.float32)
+        grad_ref[0, :, pl.ds(c * cols, cols)] = total
 
     bulk(out_x, x_ref, owners - 1, x_send, x_recv.at[0]).wait_send()
     bulk(lab_s, lab_r, owners - 1, lab_send, lab_recv.at[0]).wait_send()
     bulk(lg_s, lg_r, owners - 1, lg_send, lg_recv).wait_send()
     for c in range(CHUNKS):
         core_copy(c).wait_send()
-        for way in range(2):
-            first_leg(c, way).wait_send()
-            second_leg(c, way).wait_send()
+        for d in range(1, chips):
+            link_copy(c, d).wait_send()
 
 
 def shards(owners, groups, features, scenario_ids, labels, counts, scenario_weights, shared_weights, gate_weights, tower_weights, tower_out):
@@ -386,10 +377,8 @@
             pltpu.VMEM((CHUNKS, 2, width // 2, cols), bf16),
             pltpu.VMEM((CHUNKS, width // 2, cols), bf16),
             pltpu.VMEM((CHUNKS, 2, width // 2, cols), f32),
-            pltpu.VMEM((CHUNKS, 2, 2, part, cols // 2), bf16),
-            pltpu.VMEM((CHUNKS, 2, 2, part, cols // 2), bf16),
-            pltpu.VMEM((CHUNKS, 2, part, cols // 2), bf16),
-            pltpu.VMEM((CHUNKS, 2, part, cols // 2), bf16),
+            pltpu.VMEM((CHUNKS, chips, part, cols), bf16),
+            pltpu.VMEM((CHUNKS, chips - 1, part, cols), bf16),
             dma((9,)),
             dma(()),
             dma((2,)),
@@ -400,10 +389,8 @@
             pltpu.SemaphoreType.REGULAR,
             dma((CHUNKS,)),
             dma((CHUNKS,)),
-            dma((CHUNKS, 2)),
-            dma((CHUNKS, 2)),
-            dma((CHUNKS, 2)),
-            dma((CHUNKS, 2)),
+            dma((CHUNKS, chips - 1)),
+            dma((CHUNKS, chips - 1)),
         ],
         compiler_params=pltpu.CompilerParams(collective_id=0, has_side_effects=True, vmem_limit_bytes=56 * 1024 * 1024),
     )(

time: 44.6 us -> 44.2 us (level); the launches traced: 43.8 us -> 44.1 us
  no operation moved by 1% of the time
where the time goes in v6:
time: 44.2 us; the launch traced here: 44.1 us
  Pallas kernels  42.1 us (95%)
  local copies, waits for them, and re-layouts  1.28 us (3%)
  between operations  0.64 us (1%)
    pallas_call x1, Pallas kernels, shards(): pl.pallas_call(functools.partial(step_kernel, owners, groups), out_shape=...  42.1 us
    unnamed x2, local copies, waits for them, and re-layouts  1.28 us

profile of v6, /device:TPU:1, one launch (start us, length us, event | category | flops | bytes accessed | tf_op | source)
XLA Modules:
  0.0 44.1 jit_solution(8614653766810033675)
XLA Ops:
  0.6 42.1 %shard_map.104 = (f32[2,256]{1,0:T(2,128)S(1)}, f32[1,16,4096]{2,1,0:T(8,128)S(1)}) custom-call(s32[1,256]{1,0:T(1,128)} %bitcast.3, s32[2,256]{1,0:T(2,128)} %labels_hbm.1, bf16[256,128]{1,0:T(8,128)(2,1)} %feats_hbm.1, s32[64]{0:T(128)} %counts_hbm.1, bf16[1,128,4096]{2,1,0:T(8,128)(2,1)} %w_hbm.1, bf16[128,4096]{1,0:T(8,128)(2,1)} %s_hbm.1, ...), custom_call_target="tpu_custom_call" | custom-call | tf_op jit(solution)/shard_map/pallas_call | solution.py:354
  42.8 0.6 %copy.13 = f32[2,256]{1,0:T(2,128)} copy(f32[2,256]{1,0:T(2,128)S(1)} %get-tuple-element.2) | data formatting | bytes 4096
  43.4 0.7 %copy.14 = f32[1,16,4096]{2,1,0:T(8,128)} copy(f32[1,16,4096]{2,1,0:T(8,128)S(1)} %get-tuple-element.3) | data formatting | bytes 524288
